TPU v7x, 32 devices: a whole 2x2x4 slice. The times are simulated.
32 devices in a mesh: rows: 8 (over z, y), cols: 4 (over x, core).
Axes of the slice: x: 2, y: 2, z: 4, core: 2. Of those that a mesh axis runs over, the one named last changes fastest.
Arguments:
- sketches: bfloat16 [2048, 16384], P('rows', 'cols'), may hold values from -6 to 6, as said below
- start_basis: bfloat16 [16384, 256], P('cols'), may hold values from -6 to 6
- shrink_index: int32 [1], replicated, may hold values from 64 to 191
Outputs:
- shrunk: float32 [256, 16384], P('rows', 'cols')
Inputs may be any that keep to these rules, and one draw needn't show every extreme that they name: `sketches`: real entries.
All inputs are finite; a program needn't handle non-finite values.
Results may differ from a plain program's by a relative error of at most 0.0028.
Values may be sent and summed in bfloat16 or wider, within the bound.
A program may use at most 64 MiB of HBM per device.

v0:
```python
import jax
import jax.numpy as jnp
from jax import lax
from jax.sharding import PartitionSpec as P

ITERS = 3


def project(sketches, basis_bf):
    partial_product = jnp.dot(sketches, basis_bf, preferred_element_type=jnp.float32)
    return lax.psum(partial_product, "cols")


def orthonormal(images, gram_total):
    lower_factor = jnp.linalg.cholesky(gram_total)
    return jax.scipy.linalg.solve_triangular(lower_factor, images.T, lower=True).T


def body(sketches, start_basis, shrink_index):
    basis_bf = start_basis
    basis = start_basis.astype(jnp.float32)
    for loop_index in range(ITERS):
        projected_bf = project(sketches, basis_bf).astype(jnp.bfloat16)
        local_images = jnp.einsum(
            "lw,lk->wk", sketches, projected_bf, preferred_element_type=jnp.float32
        )
        images = lax.psum(local_images, "rows")
        gram_total = lax.psum(jnp.dot(images.T, images, precision=lax.Precision.HIGHEST), "cols")
        basis = orthonormal(images, gram_total)
        basis_bf = basis.astype(jnp.bfloat16)
    projected = project(sketches, basis_bf)
    energy = lax.psum(jnp.sum(projected * projected, axis=0), "rows")
    ordered = jnp.sort(energy)[::-1]
    threshold = lax.dynamic_index_in_dim(ordered, shrink_index[0], 0, keepdims=False)
    factor = jnp.sqrt(jnp.maximum(energy - threshold, 0.25 * threshold))
    owned_rows = basis.shape[1] // lax.axis_size("rows")
    offset = lax.axis_index("rows") * owned_rows
    columns = lax.dynamic_slice_in_dim(basis, offset, owned_rows, 1)
    scaled = columns * lax.dynamic_slice_in_dim(factor, offset, owned_rows, 0)[None, :]
    return scaled.T


def solution(mesh):
    return jax.shard_map(
        body,
        mesh=mesh,
        in_specs=(P("rows", "cols"), P("cols", None), P()),
        out_specs=P("rows", "cols"),
        check_vma=False,
    )
```

profile of v0, /device:TPU:0, one launch (start us, length us, event | category | flops | bytes accessed | tf_op | source)
XLA Modules:
  0.0 932.8 jit_solution(5308531713813557644)
XLA Ops:
  6.5 1.6 copy-done
  8.1 2.3 fusion.53
  10.4 16.3 %all-reduce.25 = bf16[256,256]{1,0:T(8,128)(2,1)S(1)} all-reduce(f32[256,256]{1,0:T(8,128)S(1)} %fusion.53), channel_id=1, replica_groups=mesh['rows'=8,'cols'=4] {'cols'}, use_global_device_ids=true, to_apply=%region_0.0 | all-reduce | flops 65536 | bytes 393216 | tf_op jit(solution)/shard_map/psum | solution.py:11
  26.7 2.7 convolution_bitcast_fusion.2
  29.5 157.0 %all-reduce.12.cloned.1.call-done = f32[4096,256]{0,1:T(8,128)} async-done(((f32[4096,256]{0,1:T(8,128)}), f32[4096,256]{0,1:T(8,128)}) %all-reduce.12.cloned.1.call-update) | async-done | bytes 4194320 | tf_op jit(solution)/shard_map/psum | solution.py:27
  186.5 7.7 fusion.54
  194.5 31.2 %all-reduce.14.cloned.1.call-done = f32[256,256]{0,1:T(8,128)} async-done(((f32[256,256]{0,1:T(8,128)}), f32[256,256]{0,1:T(8,128)}) %all-reduce.14.cloned.1.call-update) | async-done | bytes 262160 | tf_op jit(solution)/shard_map/psum | solution.py:28
  227.7 11.7 %cholesky.172 = f32[128,128]{1,0:T(8,128)S(1)} custom-call(f32[128,128]{1,0:T(8,128)S(1)} %cholesky.270), custom_call_target="Cholesky" | custom-call | tf_op jit(solution)/shard_map/jit(cholesky)/cholesky | solution.py:15
  239.5 9.8 %custom-call.15 = f32[1,128,128]{1,2,0:T(8,128)S(1)} custom-call(f32[1,128,128]{2,1,0:T(8,128)S(1)} %get-tuple-element.74), custom_call_target="InvertDiagBlocksLowerTriangular" | custom-call | tf_op jit(solution)/shard_map/jit(cholesky)/cholesky | solution.py:15
  249.8 11.7 %cholesky.189 = f32[128,128]{1,0:T(8,128)S(1)} custom-call(f32[128,128]{1,0:T(8,128)S(1)} %convolution_subtract_fusion.5), custom_call_target="Cholesky" | custom-call | tf_op jit(solution)/shard_map/jit(cholesky)/cholesky | solution.py:15
  263.6 4.3 while.6
  264.6 1.4 bitcast_dynamic-update-slice_fusion.6
  268.0 19.7 %custom-call.16 = f32[2,128,128]{1,2,0:T(8,128)S(1)} custom-call(f32[2,128,128]{2,1,0:T(8,128)S(1)} %get-tuple-element.30), custom_call_target="InvertDiagBlocksLowerTriangular" | custom-call | tf_op jit(solution)/shard_map/jit(_solve_triangular)/triangular_solve | solution.py:16
  287.6 3.6 fusion.9
  291.3 2.0 convolution_subtract_fusion.2
  293.3 1.9 fusion.33
  296.1 13.5 %all-reduce.26 = bf16[256,256]{0,1:T(8,128)(2,1)S(1)} all-reduce(f32[256,256]{0,1:T(8,128)S(1)} %fusion.14), channel_id=1, replica_groups=mesh['rows'=8,'cols'=4] {'cols'}, use_global_device_ids=true, to_apply=%region_7.0 | all-reduce | flops 65536 | bytes 393216 | tf_op jit(solution)/shard_map/psum | solution.py:11
  309.6 2.7 convolution_bitcast_fusion.1
  312.4 156.6 %all-reduce.16.cloned.1.call-done = f32[4096,256]{0,1:T(8,128)} async-done(((f32[4096,256]{0,1:T(8,128)}), f32[4096,256]{0,1:T(8,128)}) %all-reduce.16.cloned.1.call-update) | async-done | bytes 4194320 | tf_op jit(solution)/shard_map/psum | solution.py:27
  468.9 7.7 fusion.55
  476.9 31.2 %all-reduce.18.cloned.1.call-done = f32[256,256]{0,1:T(8,128)} async-done(((f32[256,256]{0,1:T(8,128)}), f32[256,256]{0,1:T(8,128)}) %all-reduce.18.cloned.1.call-update) | async-done | bytes 262160 | tf_op jit(solution)/shard_map/psum | solution.py:28
  510.2 11.7 %cholesky.206 = f32[128,128]{1,0:T(8,128)S(1)} custom-call(f32[128,128]{1,0:T(8,128)S(1)} %cholesky.273), custom_call_target="Cholesky" | custom-call | tf_op jit(solution)/shard_map/jit(cholesky)/cholesky | solution.py:15
  521.9 9.8 %custom-call.17 = f32[1,128,128]{1,2,0:T(8,128)S(1)} custom-call(f32[1,128,128]{2,1,0:T(8,128)S(1)} %get-tuple-element.70), custom_call_target="InvertDiagBlocksLowerTriangular" | custom-call | tf_op jit(solution)/shard_map/jit(cholesky)/cholesky | solution.py:15
  532.2 11.7 %cholesky.223 = f32[128,128]{1,0:T(8,128)S(1)} custom-call(f32[128,128]{1,0:T(8,128)S(1)} %convolution_subtract_fusion.4), custom_call_target="Cholesky" | custom-call | tf_op jit(solution)/shard_map/jit(cholesky)/cholesky | solution.py:15
  546.6 4.2 while.7
  550.8 19.7 %custom-call.18 = f32[2,128,128]{1,2,0:T(8,128)S(1)} custom-call(f32[2,128,128]{2,1,0:T(8,128)S(1)} %get-tuple-element.31), custom_call_target="InvertDiagBlocksLowerTriangular" | custom-call | tf_op jit(solution)/shard_map/jit(_solve_triangular)/triangular_solve | solution.py:16
  570.4 3.7 fusion.7
  574.1 2.0 convolution_subtract_fusion.1
  576.1 1.9 fusion.29
  578.9 13.5 %all-reduce.27 = bf16[256,256]{0,1:T(8,128)(2,1)S(1)} all-reduce(f32[256,256]{0,1:T(8,128)S(1)} %fusion.15), channel_id=1, replica_groups=mesh['rows'=8,'cols'=4] {'cols'}, use_global_device_ids=true, to_apply=%region_10.0 | all-reduce | flops 65536 | bytes 393216 | tf_op jit(solution)/shard_map/psum | solution.py:11
  592.4 2.7 convolution_bitcast_fusion
  595.2 156.6 %all-reduce.20.cloned.1.call-done = f32[4096,256]{0,1:T(8,128)} async-done(((f32[4096,256]{0,1:T(8,128)}), f32[4096,256]{0,1:T(8,128)}) %all-reduce.20.cloned.1.call-update) | async-done | bytes 4194320 | tf_op jit(solution)/shard_map/psum | solution.py:27
  751.8 7.7 fusion.56
  759.9 31.0 %all-reduce.22.cloned.1.call-done = f32[256,256]{0,1:T(8,128)} async-done(((f32[256,256]{0,1:T(8,128)}), f32[256,256]{0,1:T(8,128)}) %all-reduce.22.cloned.1.call-update) | async-done | bytes 262160 | tf_op jit(solution)/shard_map/psum | solution.py:28
  793.0 11.7 %cholesky.240 = f32[128,128]{1,0:T(8,128)S(1)} custom-call(f32[128,128]{1,0:T(8,128)S(1)} %cholesky.276), custom_call_target="Cholesky" | custom-call | tf_op jit(solution)/shard_map/jit(cholesky)/cholesky | solution.py:15
  804.8 9.8 %custom-call.19 = f32[1,128,128]{1,2,0:T(8,128)S(1)} custom-call(f32[1,128,128]{2,1,0:T(8,128)S(1)} %get-tuple-element.66), custom_call_target="InvertDiagBlocksLowerTriangular" | custom-call | tf_op jit(solution)/shard_map/jit(cholesky)/cholesky | solution.py:15
  815.1 11.7 %cholesky.257 = f32[128,128]{1,0:T(8,128)S(1)} custom-call(f32[128,128]{1,0:T(8,128)S(1)} %convolution_subtract_fusion.3), custom_call_target="Cholesky" | custom-call | tf_op jit(solution)/shard_map/jit(cholesky)/cholesky | solution.py:15
  829.4 4.1 while.8
  830.2 1.4 bitcast_dynamic-update-slice_fusion.8
  833.6 19.7 %custom-call.20 = f32[2,128,128]{1,2,0:T(8,128)S(1)} custom-call(f32[2,128,128]{2,1,0:T(8,128)S(1)} %get-tuple-element.32), custom_call_target="InvertDiagBlocksLowerTriangular" | custom-call | tf_op jit(solution)/shard_map/jit(_solve_triangular)/triangular_solve | solution.py:16
  853.3 3.6 fusion.5
  856.9 1.9 convolution_subtract_fusion
  858.9 1.9 fusion.25
  862.1 1.5 fusion.11
  864.3 31.8 %all-reduce.24.cloned.1.call-done = f32[256,256]{0,1:T(8,128)} async-done(((f32[256,256]{0,1:T(8,128)}), f32[256,256]{0,1:T(8,128)}) %all-reduce.24.cloned.1.call-update) | async-done | bytes 262160 | tf_op jit(solution)/shard_map/psum | solution.py:11
  897.1 21.4 %psum.87 = f32[256]{0:T(256)S(1)} all-reduce(f32[256]{0:T(256)S(1)} %multiply_reduce_fusion), channel_id=1, replica_groups=mesh['rows'=8,'cols'=4] {'rows'}, use_global_device_ids=true, to_apply=%region_15.18 | all-reduce | flops 256 | bytes 2048 | tf_op jit(solution)/shard_map/psum | solution.py:32
  918.5 3.3 sort.15
  923.8 1.9 fusion.17
  (86 shorter events, 27.0 us)
Async XLA Ops:
  6.5 1.6 copy-start
  6.5 180.0 %all-reduce.12.cloned.1.call-start = ((), (), s32[]{:S(2)}) async-start(), calls=%async_computation | async-start | bytes 8388608 | tf_op jit(solution)/shard_map/psum | solution.py:27
  29.4 196.2 %all-reduce.14.cloned.1.call-start = ((), (), s32[]{:S(2)}) async-start(), calls=%async_computation.1 | async-start | bytes 524288 | tf_op jit(solution)/shard_map/psum | solution.py:28
  194.2 274.7 %all-reduce.16.cloned.1.call-start = ((), (), s32[]{:S(2)}) async-start(), calls=%async_computation.2 | async-start | bytes 8388608 | tf_op jit(solution)/shard_map/psum | solution.py:27
  287.6 3.7 copy-start.1
  312.3 195.7 %all-reduce.18.cloned.1.call-start = ((), (), s32[]{:S(2)}) async-start(), calls=%async_computation.3 | async-start | bytes 524288 | tf_op jit(solution)/shard_map/psum | solution.py:28
  476.7 275.1 %all-reduce.20.cloned.1.call-start = ((), (), s32[]{:S(2)}) async-start(), calls=%async_computation.4 | async-start | bytes 8388608 | tf_op jit(solution)/shard_map/psum | solution.py:27
  570.4 3.7 copy-start.3
  595.1 195.8 %all-reduce.22.cloned.1.call-start = ((), (), s32[]{:S(2)}) async-start(), calls=%async_computation.5 | async-start | bytes 524288 | tf_op jit(solution)/shard_map/psum | solution.py:28
  759.5 136.6 %all-reduce.24.cloned.1.call-start = ((), (), s32[]{:S(2)}) async-start(), calls=%async_computation.6 | async-start | bytes 524288 | tf_op jit(solution)/shard_map/psum | solution.py:11
  853.2 3.7 copy-start.2
  856.9 3.9 copy-start.4
  860.8 1.3 copy-start.5
Sparse Core Ops, SparseCore 0:
  29.6 156.8 all-reduce.11
  194.3 31.2 all-reduce.13
  312.5 156.4 all-reduce.15
  476.8 31.2 all-reduce.17
  595.3 156.4 all-reduce.19
  759.6 31.2 all-reduce.21
  863.8 32.2 all-reduce.23
where the time goes:
time: 938 us; the launch traced here: 933 us
  waiting for transfers between devices  595 us (63%)
  other arithmetic  172 us (18%)
  blocking collectives  64.6 us (7%)
  matrix products  60.7 us (6%)
  between operations  19.2 us (2%)
  local copies, waits for them, and re-layouts  18.7 us (2%)
    psum x3, waiting for transfers between devices, body(): images = lax.psum(local_images, 'rows')  470 us
    another operation x20, other arithmetic, orthonormal(): lower_factor = jnp.linalg.cholesky(gram_total)  103 us
    psum x3, waiting for transfers between devices, body(): lax.psum(jnp.dot(images.T, images, precision=lax.Precision.HIGHEST), 'cols')  93.3 us
    another operation x7, other arithmetic, orthonormal(): jax.scipy.linalg.solve_triangular(lower_factor, images.T, lower=True)  59.1 us
    psum x3, blocking collectives, project(): return lax.psum(partial_product, 'cols')  43.3 us
    psum x1, waiting for transfers between devices, project(): return lax.psum(partial_product, 'cols')  31.8 us
    dot_general x3, matrix products, body(): jnp.dot(images.T, images, precision=lax.Precision.HIGHEST)  23.1 us
    another operation x9, matrix products, orthonormal(): jax.scipy.linalg.solve_triangular(lower_factor, images.T, lower=True)  22.6 us
  transfers between devices with their start and end apart: 7, of which 7 were waited for; matrix products, arithmetic and copies ran while one was open for 0% of the time, Pallas kernels for 0%

commit v1 on v0

v1 whole, which is shorter than its diff:
```python
import jax
import jax.numpy as jnp
from jax import lax
from jax.sharding import PartitionSpec as P

ITERS = 3
AXES = ("rows", "cols")
HIGHEST = lax.Precision.HIGHEST


def pieces(values):
    high = lax.reduce_precision(values, 8, 7)
    rest = values - high
    middle = lax.reduce_precision(rest, 8, 7)
    low = rest - middle
    return [part.astype(jnp.bfloat16) for part in (high, middle, low)]


def apply_sketches(strip, images):
    stacked = jnp.concatenate(pieces(images), axis=1)
    products = jnp.dot(strip, stacked, preferred_element_type=jnp.float32)
    high, middle, low = jnp.split(products, 3, axis=1)
    return high + (middle + low)


def all_sum(values):
    return lax.psum(values, AXES)


def inverse_factor(gram_total):
    lower_factor = jnp.linalg.cholesky(gram_total)
    identity = jnp.eye(gram_total.shape[0], dtype=jnp.float32)
    return jax.scipy.linalg.solve_triangular(lower_factor, identity, lower=True)


def body(sketches, start_basis, shrink_index):
    size = lax.axis_size("rows")
    strip = lax.all_to_all(sketches, "rows", split_axis=1, concat_axis=0, tiled=True)
    width = start_basis.shape[0] // size
    own_basis = lax.dynamic_slice_in_dim(start_basis, lax.axis_index("rows") * width, width, 0)
    projected = all_sum(jnp.dot(strip, own_basis, preferred_element_type=jnp.float32))
    for loop_index in range(ITERS):
        projected_bf = projected.astype(jnp.bfloat16)
        images = jnp.einsum("lw,lk->wk", strip, projected_bf, preferred_element_type=jnp.float32)
        raw = all_sum(apply_sketches(strip, images))
        gram_total = jnp.dot(projected_bf.astype(jnp.float32).T, raw, precision=HIGHEST)
        gram_total = 0.5 * (gram_total + gram_total.T)
        inverse = inverse_factor(gram_total)
        projected = jnp.dot(raw, inverse.T, precision=HIGHEST)
    energy = jnp.sum(projected * projected, axis=0)
    ordered = jnp.sort(energy)[::-1]
    threshold = lax.dynamic_index_in_dim(ordered, shrink_index[0], 0, keepdims=False)
    factor = jnp.sqrt(jnp.maximum(energy - threshold, 0.25 * threshold))
    scaled = jnp.dot(inverse * factor[:, None], images.T, precision=HIGHEST)
    return lax.all_to_all(scaled, "rows", split_axis=0, concat_axis=1, tiled=True)


def solution(mesh):
    return jax.shard_map(
        body,
        mesh=mesh,
        in_specs=(P("rows", "cols"), P("cols", None), P()),
        out_specs=P("rows", "cols"),
        check_vma=False,
    )
```

time: 938 us -> 802 us (0.86)
  waiting for transfers between devices: 595 us -> 448 us
  matrix products: 60.7 us -> 44.7 us
  blocking collectives: 64.6 us -> 76.4 us
    psum x7 -> x3, waiting for transfers between devices: 595 us -> 400 us  [all_sum(): return lax.psum(values, AXES)]
    all_to_all x0 -> x1, waiting for transfers between devices: none -> 48.3 us  [body(): lax.all_to_all(sketches, 'rows', split_axis=1, concat_axis=0, tiled=True)]
    another operation x15, matrix products: 24 us -> 4.06 us  [the longest x9 2.64 us: inverse_factor(): return jax.scipy.linalg.solve_triangular(lower_factor, identity, lower=True)]
    all_to_all x0 -> x1, blocking collectives: none -> 16.7 us  [body(): lax.all_to_all(scaled, 'rows', split_axis=0, concat_axis=1, tiled=True)]
    psum x4 -> x1, blocking collectives: 64.6 us -> 59.7 us  [all_sum(): return lax.psum(values, AXES)]
    dot_general x10 -> x14, matrix products: 36.7 us -> 40.7 us  [the longest x3 15.2 us: body(): projected = jnp.dot(raw, inverse.T, precision=HIGHEST)]
  transfers between devices with their start and end apart: 7 -> 4, of which waited for: 7 -> 4; matrix products, arithmetic and copies ran while one was open for 0% -> 0% of each run, Pallas kernels for 0% -> 0%
where the time goes in v1:
time: 802 us; the launch traced here: 797 us
  waiting for transfers between devices  448 us (56%)
  other arithmetic  176 us (22%)
  blocking collectives  76.4 us (10%)
  matrix products  44.7 us (6%)
  local copies, waits for them, and re-layouts  25.2 us (3%)
  between operations  18.9 us (2%)
    psum x3, waiting for transfers between devices, all_sum(): return lax.psum(values, AXES)  400 us
    another operation x20, other arithmetic, inverse_factor(): lower_factor = jnp.linalg.cholesky(gram_total)  104 us
    psum x1, blocking collectives, all_sum(): return lax.psum(values, AXES)  59.7 us
    another operation x7, other arithmetic, inverse_factor(): return jax.scipy.linalg.solve_triangular(lower_factor, identity, lower=True)  59.5 us
    all_to_all x1, waiting for transfers between devices, body(): lax.all_to_all(sketches, 'rows', split_axis=1, concat_axis=0, tiled=True)  48.3 us
    all_to_all x1, blocking collectives, body(): lax.all_to_all(scaled, 'rows', split_axis=0, concat_axis=1, tiled=True)  16.7 us
  transfers between devices with their start and end apart: 4, of which 4 were waited for; matrix products, arithmetic and copies ran while one was open for 0% of the time, Pallas kernels for 0%

profile of v1, /device:TPU:0, one launch (start us, length us, event | category | flops | bytes accessed | tf_op | source)
XLA Modules:
  0.0 797.4 jit_solution(12065096326215861704)
XLA Ops:
  6.5 4.3 copy.18
  10.8 7.3 all-to-all-start
  18.1 48.3 %all-to-all-done = bf16[256,8,512]{0,2,1:T(8,128)(2,1)} async-done(((bf16[256,8,512]{0,2,1:T(8,128)(2,1)}), bf16[256,8,512]{0,2,1:T(8,128)(2,1)}, u32[]{:S(2)}, u32[]{:S(2)}) %all-to-all-start) | async-done | bytes 2097184 | tf_op jit(solution)/shard_map/all_to_all | solution.py:38
  66.4 3.9 copy.19
  70.4 3.6 convolution_bitcast_fusion.3
  74.0 59.7 %all-reduce.11 = bf16[2048,256]{0,1:T(8,128)(2,1)S(1)} all-reduce(f32[2048,256]{0,1:T(8,128)} %convolution_bitcast_fusion.3), channel_id=1, replica_groups=mesh['rows'=8,'cols'=4] {'rows','cols'}, use_global_device_ids=true, to_apply=%region_0.0 | all-reduce | flops 524288 | bytes 3145728 | tf_op jit(solution)/shard_map/psum | solution.py:27
  133.8 2.5 reduce-precision_convert_fusion.5
  136.3 1.8 convolution_bitcast_fusion.2
  138.1 1.8 fusion.2
  140.4 133.4 %all-reduce.6.cloned.1.call-done = f32[2048,256]{0,1:T(8,128)} async-done(((f32[2048,256]{0,1:T(8,128)}), f32[2048,256]{0,1:T(8,128)}) %all-reduce.6.cloned.1.call-update) | async-done | bytes 2097168 | tf_op jit(solution)/shard_map/psum | solution.py:27
  273.7 3.5 fusion.84
  277.2 1.1 copy.20
  279.5 11.7 %cholesky.172 = f32[128,128]{1,0:T(8,128)S(1)} custom-call(f32[128,128]{1,0:T(8,128)S(1)} %cholesky.270), custom_call_target="Cholesky" | custom-call | tf_op jit(solution)/shard_map/jit(cholesky)/cholesky | solution.py:31
  291.2 9.8 %custom-call.15 = f32[1,128,128]{1,2,0:T(8,128)S(1)} custom-call(f32[1,128,128]{2,1,0:T(8,128)S(1)} %get-tuple-element.83), custom_call_target="InvertDiagBlocksLowerTriangular" | custom-call | tf_op jit(solution)/shard_map/jit(cholesky)/cholesky | solution.py:31
  301.5 11.7 %cholesky.189 = f32[128,128]{1,0:T(8,128)S(1)} custom-call(f32[128,128]{1,0:T(8,128)S(1)} %convolution_subtract_fusion.5), custom_call_target="Cholesky" | custom-call | tf_op jit(solution)/shard_map/jit(cholesky)/cholesky | solution.py:31
  315.3 4.5 while.6
  316.5 1.4 bitcast_dynamic-update-slice_fusion.6
  318.4 1.4 bitcast_dynamic-update-slice_fusion.6
  319.8 19.7 %custom-call.16 = f32[2,128,128]{1,2,0:T(8,128)S(1)} custom-call(f32[2,128,128]{2,1,0:T(8,128)S(1)} %get-tuple-element.30), custom_call_target="InvertDiagBlocksLowerTriangular" | custom-call | tf_op jit(solution)/shard_map/jit(_solve_triangular)/triangular_solve | solution.py:33
  340.4 5.1 convolution_convert_fusion.1
  346.3 1.8 convolution_bitcast_fusion.1
  348.1 1.8 fusion.1
  350.2 133.4 %all-reduce.8.cloned.1.call-done = f32[2048,256]{0,1:T(8,128)} async-done(((f32[2048,256]{0,1:T(8,128)}), f32[2048,256]{0,1:T(8,128)}) %all-reduce.8.cloned.1.call-update) | async-done | bytes 2097168 | tf_op jit(solution)/shard_map/psum | solution.py:27
  483.5 3.7 fusion.82
  487.3 1.1 copy.22
  489.5 11.7 %cholesky.206 = f32[128,128]{1,0:T(8,128)S(1)} custom-call(f32[128,128]{1,0:T(8,128)S(1)} %cholesky.273), custom_call_target="Cholesky" | custom-call | tf_op jit(solution)/shard_map/jit(cholesky)/cholesky | solution.py:31
  501.3 9.8 %custom-call.17 = f32[1,128,128]{1,2,0:T(8,128)S(1)} custom-call(f32[1,128,128]{2,1,0:T(8,128)S(1)} %get-tuple-element.79), custom_call_target="InvertDiagBlocksLowerTriangular" | custom-call | tf_op jit(solution)/shard_map/jit(cholesky)/cholesky | solution.py:31
  511.6 11.7 %cholesky.223 = f32[128,128]{1,0:T(8,128)S(1)} custom-call(f32[128,128]{1,0:T(8,128)S(1)} %convolution_subtract_fusion.4), custom_call_target="Cholesky" | custom-call | tf_op jit(solution)/shard_map/jit(cholesky)/cholesky | solution.py:31
  526.0 3.9 while.7
  526.6 1.4 bitcast_dynamic-update-slice_fusion.7
  528.5 1.4 bitcast_dynamic-update-slice_fusion.7
  529.9 19.9 %custom-call.18 = f32[2,128,128]{1,2,0:T(8,128)S(1)} custom-call(f32[2,128,128]{2,1,0:T(8,128)S(1)} %get-tuple-element.31), custom_call_target="InvertDiagBlocksLowerTriangular" | custom-call | tf_op jit(solution)/shard_map/jit(_solve_triangular)/triangular_solve | solution.py:33
  550.7 5.1 convolution_convert_fusion
  555.8 1.5 reduce-precision_convert_fusion.1
  557.3 1.8 convolution_bitcast_fusion
  559.2 1.8 fusion
  561.7 132.9 %all-reduce.10.cloned.1.call-done = f32[2048,256]{0,1:T(8,128)} async-done(((f32[2048,256]{0,1:T(8,128)}), f32[2048,256]{0,1:T(8,128)}) %all-reduce.10.cloned.1.call-update) | async-done | bytes 2097168 | tf_op jit(solution)/shard_map/psum | solution.py:27
  694.5 3.8 fusion.83
  700.6 11.7 %cholesky.240 = f32[128,128]{1,0:T(8,128)S(1)} custom-call(f32[128,128]{1,0:T(8,128)S(1)} %cholesky.276), custom_call_target="Cholesky" | custom-call | tf_op jit(solution)/shard_map/jit(cholesky)/cholesky | solution.py:31
  712.3 10.2 %custom-call.19 = f32[1,128,128]{1,2,0:T(8,128)S(1)} custom-call(f32[1,128,128]{2,1,0:T(8,128)S(1)} %get-tuple-element.75), custom_call_target="InvertDiagBlocksLowerTriangular" | custom-call | tf_op jit(solution)/shard_map/jit(cholesky)/cholesky | solution.py:31
  723.0 11.7 %cholesky.257 = f32[128,128]{1,0:T(8,128)S(1)} custom-call(f32[128,128]{1,0:T(8,128)S(1)} %convolution_subtract_fusion.3), custom_call_target="Cholesky" | custom-call | tf_op jit(solution)/shard_map/jit(cholesky)/cholesky | solution.py:31
  737.4 3.9 while.8
  738.0 1.3 bitcast_dynamic-update-slice_fusion.8
  739.9 1.3 bitcast_dynamic-update-slice_fusion.8
  741.3 19.8 %custom-call.20 = f32[2,128,128]{1,2,0:T(8,128)S(1)} custom-call(f32[2,128,128]{2,1,0:T(8,128)S(1)} %get-tuple-element.32), custom_call_target="InvertDiagBlocksLowerTriangular" | custom-call | tf_op jit(solution)/shard_map/jit(_solve_triangular)/triangular_solve | solution.py:33
  762.0 5.0 fusion.3
  767.1 3.3 sort.15
  773.2 16.7 %all_to_all.38 = f32[8,32,512]{2,1,0:T(8,128)S(1)} all-to-all(f32[8,32,512]{2,1,0:T(8,128)S(1)} %bitcast.164), channel_id=1, replica_groups=mesh['rows'=8,'cols'=4] {'rows'}, dimensions={0} | all-to-all | bytes 1048576 | tf_op jit(solution)/shard_map/all_to_all | solution.py:55
  (86 shorter events, 20.3 us)
Async XLA Ops:
  6.5 63.8 %copy-start = (bf16[4096,256]{1,0:T(8,128)(2,1)S(1)}, bf16[4096,256]{1,0:T(8,128)(2,1)}, u32[]{:S(2)}) copy-start(bf16[4096,256]{1,0:T(8,128)(2,1)} %param.7) | copy-start | bytes 6291460
  10.8 55.7 %all-to-all-start = ((bf16[256,8,512]{0,2,1:T(8,128)(2,1)}), bf16[256,8,512]{0,2,1:T(8,128)(2,1)}, u32[]{:S(2)}, u32[]{:S(2)}) async-start(bf16[256,8,512]{0,2,1:T(8,128)(2,1)} %bitcast.163), calls=%async_computation | async-start | bytes 4194304 | tf_op jit(solution)/shard_map/all_to_all | solution.py:38
  18.1 255.6 %all-reduce.6.cloned.1.call-start = ((), (), s32[]{:S(2)}) async-start(), calls=%async_computation.2 | async-start | bytes 4194304 | tf_op jit(solution)/shard_map/psum | solution.py:27
  133.8 2.5 copy-start.1
  140.0 343.6 %all-reduce.8.cloned.1.call-start = ((), (), s32[]{:S(2)}) async-start(), calls=%async_computation.3 | async-start | bytes 4194304 | tf_op jit(solution)/shard_map/psum | solution.py:27
  339.8 5.7 copy-start.2
  350.0 344.6 %all-reduce.10.cloned.1.call-start = ((), (), s32[]{:S(2)}) async-start(), calls=%async_computation.4 | async-start | bytes 4194304 | tf_op jit(solution)/shard_map/psum | solution.py:27
  550.1 5.7 copy-start.3
  737.4 35.2 %copy-start.4 = (f32[256,512]{1,0:T(8,128)S(1)}, f32[256,512]{1,0:T(8,128)}, u32[]{:S(2)}) copy-start(f32[256,512]{1,0:T(8,128)} %get-tuple-element.88) | copy-start | bytes 1572868
Sparse Core Ops, SparseCore 0:
  140.1 133.5 all-reduce.5
  350.1 133.4 all-reduce.7
  561.1 133.3 all-reduce.9

commit v2 on v1

--- a/solution.py
+++ b/solution.py
@@ -1,6 +1,10 @@
+import functools
+
 import jax
 import jax.numpy as jnp
 from jax import lax
+from jax.experimental import pallas as pl
+from jax.experimental.pallas import tpu as pltpu
 from jax.sharding import PartitionSpec as P
 
 ITERS = 3
@@ -23,8 +27,113 @@
     return high + (middle + low)
 
 
+def path_orders(sizes):
+    cols_bits = [("cols", 1 << bit) for bit in range(sizes["cols"].bit_length() - 1)]
+    rows_bits = [("rows", 1 << bit) for bit in range(sizes["rows"].bit_length() - 1)]
+    first = cols_bits + rows_bits
+    second = cols_bits[:1] + rows_bits[:1] + cols_bits[1:] + rows_bits[1:]
+    return [first, second]
+
+
+def sum_kernel(orders, x_ref, out_ref, partial, arrived, send_sems, recv_sems):
+    index = {axis: lax.axis_index(axis) for axis in AXES}
+    stages = len(orders[0])
+    rows = x_ref.shape[0] // len(orders)
+
+    def side_of(axis, step):
+        return lax.rem(index[axis] // step, 2)
+
+    def partner_of(axis, step):
+        return {axis: index[axis] + step * (1 - 2 * side_of(axis, step))}
+
+    barrier = pltpu.get_barrier_semaphore()
+    for axis, step in orders[0]:
+        pl.semaphore_signal(
+            barrier, inc=1, device_id=partner_of(axis, step), device_id_type=pl.DeviceIdType.MESH
+        )
+    pl.semaphore_wait(barrier, stages)
+
+    copies = []
+
+    def send(path, phase, stage, src, dst):
+        copy = pltpu.make_async_remote_copy(
+            src_ref=src,
+            dst_ref=dst,
+            send_sem=send_sems.at[path, phase, stage],
+            recv_sem=recv_sems.at[path, phase, stage],
+            device_id=partner_of(*orders[path][stage]),
+            device_id_type=pl.DeviceIdType.MESH,
+        )
+        copy.start()
+        copies.append(copy)
+        return copy
+
+    def span(start, size):
+        return pl.ds(pl.multiple_of(start, 8), size)
+
+    lows = [path * rows for path in range(len(orders))]
+    trail = [[] for _ in orders]
+    pending = [None for _ in orders]
+
+    def halve(path, stage):
+        half = rows >> (stage + 1)
+        side = side_of(*orders[path][stage])
+        source = x_ref if stage == 0 else partial
+        slot = path * rows + rows - (rows >> stage)
+        pending[path] = send(
+            path, 0, stage,
+            source.at[span(lows[path] + (1 - side) * half, half), :],
+            arrived.at[slot : slot + half, :],
+        )
+        trail[path].append(lows[path])
+        lows[path] = lows[path] + side * half
+
+    for path in range(len(orders)):
+        halve(path, 0)
+    for stage in range(stages):
+        half = rows >> (stage + 1)
+        for path in range(len(orders)):
+            pending[path].wait_recv()
+            slot = path * rows + rows - (rows >> stage)
+            own = span(lows[path], half)
+            source = x_ref if stage == 0 else partial
+            target = out_ref if stage == stages - 1 else partial
+            target[own, :] = source[own, :] + arrived[slot : slot + half, :]
+            if stage + 1 < stages:
+                halve(path, stage + 1)
+            else:
+                own_rows = out_ref.at[own, :]
+                pending[path] = send(path, 1, stage, own_rows, own_rows)
+    for stage in reversed(range(stages)):
+        for path in range(len(orders)):
+            pending[path].wait_recv()
+            if stage > 0:
+                held = out_ref.at[span(trail[path][stage], rows >> stage), :]
+                pending[path] = send(path, 1, stage - 1, held, held)
+    for copy in copies:
+        copy.wait_send()
+
+
 def all_sum(values):
-    return lax.psum(values, AXES)
+    sizes = {axis: lax.axis_size(axis) for axis in AXES}
+    orders = path_orders(sizes)
+    stages = len(orders[0])
+    return pl.pallas_call(
+        functools.partial(sum_kernel, orders),
+        out_shape=jax.ShapeDtypeStruct(values.shape, jnp.float32),
+        in_specs=[pl.BlockSpec(memory_space=pltpu.VMEM)],
+        out_specs=pl.BlockSpec(memory_space=pltpu.VMEM),
+        scratch_shapes=[
+            pltpu.VMEM(values.shape, jnp.float32),
+            pltpu.VMEM(values.shape, jnp.float32),
+            pltpu.SemaphoreType.DMA((len(orders), 2, stages)),
+            pltpu.SemaphoreType.DMA((len(orders), 2, stages)),
+        ],
+        compiler_params=pltpu.CompilerParams(
+            collective_id=0, has_side_effects=True, vmem_limit_bytes=48 << 20
+        ),
+        name="all_sum",
+    )(values)
 
 
 def inverse_factor(gram_total):

time: 802 us -> 489 us (0.61)
  waiting for transfers between devices: 448 us -> 47.7 us
  Pallas kernels: 0 us -> 172 us
  blocking collectives: 76.4 us -> 20.1 us
  matrix products: 44.7 us -> 30.3 us
  between operations: 18.9 us -> 6.24 us
    psum x3 -> x0, waiting for transfers between devices: 400 us -> none  [all_sum(): return lax.psum(values, AXES)]
    pallas_call x0 -> x4, Pallas kernels: none -> 172 us  [all_sum(): pl.pallas_call(functools.partial(sum_kernel, orders), out_shape=jax.Shape...]
    psum x1 -> x0, blocking collectives: 59.7 us -> none  [all_sum(): return lax.psum(values, AXES)]
  transfers between devices with their start and end apart: 4 -> 1, of which waited for: 4 -> 1; matrix products, arithmetic and copies ran while one was open for 0% -> 0% of each run, Pallas kernels for 0% -> 0%
where the time goes in v2:
time: 489 us; the launch traced here: 479 us
  Pallas kernels  172 us (35%)
  other arithmetic  169 us (35%)
  waiting for transfers between devices  47.7 us (10%)
  matrix products  30.3 us (6%)
  local copies, waits for them, and re-layouts  26.6 us (5%)
  blocking collectives  20.1 us (4%)
  starting transfers between devices  7.31 us (1%)
  between operations  6.24 us (1%)
    pallas_call x4, Pallas kernels, all_sum(): pl.pallas_call(functools.partial(sum_kernel, orders), out_shape=jax.Shape...  172 us
    another operation x20, other arithmetic, inverse_factor(): lower_factor = jnp.linalg.cholesky(gram_total)  104 us
    another operation x7, other arithmetic, inverse_factor(): return jax.scipy.linalg.solve_triangular(lower_factor, identity, lower=True)  59.3 us
    all_to_all x1, waiting for transfers between devices, body(): lax.all_to_all(sketches, 'rows', split_axis=1, concat_axis=0, tiled=True)  47.7 us
    all_to_all x1, blocking collectives, body(): lax.all_to_all(scaled, 'rows', split_axis=0, concat_axis=1, tiled=True)  20.1 us
    another operation x22, local copies, waits for them, and re-layouts, inverse_factor(): return jax.scipy.linalg.solve_triangular(lower_factor, identity, lower=True)  12 us
    dot_general x3, matrix products, body(): projected = jnp.dot(raw, inverse.T, precision=HIGHEST)  10.4 us
  transfers between devices with their start and end apart: 1, of which 1 were waited for; matrix products, arithmetic and copies ran while one was open for 0% of the time, Pallas kernels for 0%

profile of v2, /device:TPU:0, one launch (start us, length us, event | category | flops | bytes accessed | tf_op | source)
XLA Modules:
  0.0 479.0 jit_solution(6856423292937072390)
XLA Ops:
  0.0 4.3 copy.26
  4.3 7.3 %all-to-all-start = ((bf16[256,8,512]{0,2,1:T(8,128)(2,1)}), bf16[256,8,512]{0,2,1:T(8,128)(2,1)}, u32[]{:S(2)}, u32[]{:S(2)}) async-start(bf16[256,8,512]{0,2,1:T(8,128)(2,1)} %bitcast.161), calls=%async_computation | async-start | bytes 4194304 | tf_op jit(solution)/shard_map/all_to_all | solution.py:147
  12.3 47.7 %all-to-all-done = bf16[256,8,512]{0,2,1:T(8,128)(2,1)} async-done(((bf16[256,8,512]{0,2,1:T(8,128)(2,1)}), bf16[256,8,512]{0,2,1:T(8,128)(2,1)}, u32[]{:S(2)}, u32[]{:S(2)}) %all-to-all-start) | async-done | bytes 2097184 | tf_op jit(solution)/shard_map/all_to_all | solution.py:147
  59.9 3.9 copy.27
  63.8 2.3 convolution_bitcast_fusion.3.x_ref
  66.2 42.7 %all_sum.4 = f32[2048,256]{1,0:T(8,128)S(1)} custom-call(f32[2048,256]{1,0:T(8,128)S(1)} %convolution_bitcast_fusion.3.x_ref), custom_call_target="tpu_custom_call" | custom-call | tf_op jit(solution)/shard_map/all_sum/pallas_call | solution.py:121
  108.9 0.8 reduce-precision_convert_fusion.5
  109.7 1.8 convolution_bitcast_fusion.2
  111.9 42.6 %all_sum.5 = f32[2048,256]{1,0:T(8,128)S(1)} custom-call(f32[2048,256]{1,0:T(8,128)S(1)} %fusion.2.x_ref), custom_call_target="tpu_custom_call" | custom-call | tf_op jit(solution)/shard_map/all_sum/pallas_call | solution.py:121
  154.6 1.3 copy-done.1
  155.9 1.4 fusion.22
  157.7 11.7 %cholesky.172 = f32[128,128]{1,0:T(8,128)S(1)} custom-call(f32[128,128]{1,0:T(8,128)S(1)} %cholesky.270), custom_call_target="Cholesky" | custom-call | tf_op jit(solution)/shard_map/jit(cholesky)/cholesky | solution.py:140
  169.5 9.8 %custom-call.15 = f32[1,128,128]{1,2,0:T(8,128)S(1)} custom-call(f32[1,128,128]{2,1,0:T(8,128)S(1)} %get-tuple-element.83), custom_call_target="InvertDiagBlocksLowerTriangular" | custom-call | tf_op jit(solution)/shard_map/jit(cholesky)/cholesky | solution.py:140
  179.7 12.0 %cholesky.189 = f32[128,128]{1,0:T(8,128)S(1)} custom-call(f32[128,128]{1,0:T(8,128)S(1)} %convolution_subtract_fusion.5), custom_call_target="Cholesky" | custom-call | tf_op jit(solution)/shard_map/jit(cholesky)/cholesky | solution.py:140
  193.9 4.1 while.6
  194.6 1.3 bitcast_dynamic-update-slice_fusion.6
  196.7 1.3 bitcast_dynamic-update-slice_fusion.6
  198.0 19.7 %custom-call.16 = f32[2,128,128]{1,2,0:T(8,128)S(1)} custom-call(f32[2,128,128]{2,1,0:T(8,128)S(1)} %get-tuple-element.30), custom_call_target="InvertDiagBlocksLowerTriangular" | custom-call | tf_op jit(solution)/shard_map/jit(_solve_triangular)/triangular_solve | solution.py:142
  218.6 3.5 convolution_convert_fusion.1
  222.1 0.8 reduce-precision_convert_fusion.3
  222.9 1.8 convolution_bitcast_fusion.1
  225.1 43.7 %all_sum.6 = f32[2048,256]{1,0:T(8,128)S(1)} custom-call(f32[2048,256]{1,0:T(8,128)S(1)} %fusion.1.x_ref), custom_call_target="tpu_custom_call" | custom-call | tf_op jit(solution)/shard_map/all_sum/pallas_call | solution.py:121
  268.8 1.3 copy-done.3
  270.1 1.5 fusion.82
  272.0 11.7 %cholesky.206 = f32[128,128]{1,0:T(8,128)S(1)} custom-call(f32[128,128]{1,0:T(8,128)S(1)} %cholesky.273), custom_call_target="Cholesky" | custom-call | tf_op jit(solution)/shard_map/jit(cholesky)/cholesky | solution.py:140
  283.7 10.0 %custom-call.17 = f32[1,128,128]{1,2,0:T(8,128)S(1)} custom-call(f32[1,128,128]{2,1,0:T(8,128)S(1)} %get-tuple-element.79), custom_call_target="InvertDiagBlocksLowerTriangular" | custom-call | tf_op jit(solution)/shard_map/jit(cholesky)/cholesky | solution.py:140
  294.2 11.7 %cholesky.223 = f32[128,128]{1,0:T(8,128)S(1)} custom-call(f32[128,128]{1,0:T(8,128)S(1)} %convolution_subtract_fusion.4), custom_call_target="Cholesky" | custom-call | tf_op jit(solution)/shard_map/jit(cholesky)/cholesky | solution.py:140
  308.7 4.1 while.7
  309.3 1.4 bitcast_dynamic-update-slice_fusion.7
  311.3 1.4 bitcast_dynamic-update-slice_fusion.7
  312.8 19.9 %custom-call.18 = f32[2,128,128]{1,2,0:T(8,128)S(1)} custom-call(f32[2,128,128]{2,1,0:T(8,128)S(1)} %get-tuple-element.31), custom_call_target="InvertDiagBlocksLowerTriangular" | custom-call | tf_op jit(solution)/shard_map/jit(_solve_triangular)/triangular_solve | solution.py:142
  333.6 3.5 convolution_convert_fusion
  337.1 1.5 reduce-precision_convert_fusion.1
  338.6 1.8 convolution_bitcast_fusion
  340.9 42.8 %all_sum.7 = f32[2048,256]{1,0:T(8,128)S(1)} custom-call(f32[2048,256]{1,0:T(8,128)S(1)} %fusion.x_ref), custom_call_target="tpu_custom_call" | custom-call | tf_op jit(solution)/shard_map/all_sum/pallas_call | solution.py:121
  383.7 1.3 copy-done.2
  385.1 1.5 fusion.83
  386.9 11.7 %cholesky.240 = f32[128,128]{1,0:T(8,128)S(1)} custom-call(f32[128,128]{1,0:T(8,128)S(1)} %cholesky.276), custom_call_target="Cholesky" | custom-call | tf_op jit(solution)/shard_map/jit(cholesky)/cholesky | solution.py:140
  398.7 10.0 %custom-call.19 = f32[1,128,128]{1,2,0:T(8,128)S(1)} custom-call(f32[1,128,128]{2,1,0:T(8,128)S(1)} %get-tuple-element.75), custom_call_target="InvertDiagBlocksLowerTriangular" | custom-call | tf_op jit(solution)/shard_map/jit(cholesky)/cholesky | solution.py:140
  409.2 11.7 %cholesky.257 = f32[128,128]{1,0:T(8,128)S(1)} custom-call(f32[128,128]{1,0:T(8,128)S(1)} %convolution_subtract_fusion.3), custom_call_target="Cholesky" | custom-call | tf_op jit(solution)/shard_map/jit(cholesky)/cholesky | solution.py:140
  423.6 3.9 while.8
  424.2 1.3 bitcast_dynamic-update-slice_fusion.8
  426.1 1.3 bitcast_dynamic-update-slice_fusion.8
  427.5 19.7 %custom-call.20 = f32[2,128,128]{1,2,0:T(8,128)S(1)} custom-call(f32[2,128,128]{2,1,0:T(8,128)S(1)} %get-tuple-element.32), custom_call_target="InvertDiagBlocksLowerTriangular" | custom-call | tf_op jit(solution)/shard_map/jit(_solve_triangular)/triangular_solve | solution.py:142
  448.0 3.4 fusion.3
  451.5 3.3 sort.15
  457.6 20.1 %all_to_all.38 = f32[8,32,512]{2,1,0:T(8,128)S(1)} all-to-all(f32[8,32,512]{2,1,0:T(8,128)S(1)} %bitcast.162), channel_id=1, replica_groups=mesh['rows'=8,'cols'=4] {'rows'}, dimensions={0} | all-to-all | bytes 1048576 | tf_op jit(solution)/shard_map/all_to_all | solution.py:164
  477.7 0.8 copy.43
  (86 shorter events, 16.0 us)
Async XLA Ops:
  0.0 63.8 %copy-start = (bf16[4096,256]{1,0:T(8,128)(2,1)S(1)}, bf16[4096,256]{1,0:T(8,128)(2,1)}, u32[]{:S(2)}) copy-start(bf16[4096,256]{1,0:T(8,128)(2,1)} %param.7) | copy-start | bytes 6291460
  4.3 55.7 %all-to-all-start = ((bf16[256,8,512]{0,2,1:T(8,128)(2,1)}), bf16[256,8,512]{0,2,1:T(8,128)(2,1)}, u32[]{:S(2)}, u32[]{:S(2)}) async-start(bf16[256,8,512]{0,2,1:T(8,128)(2,1)} %bitcast.161), calls=%async_computation | async-start | bytes 4194304 | tf_op jit(solution)/shard_map/all_to_all | solution.py:147
  66.2 42.7 %copy-start.4 = (bf16[8,256,512]{2,1,0:T(8,128)(2,1)S(1)}, bf16[8,256,512]{2,1,0:T(8,128)(2,1)}, u32[]{:S(2)}) copy-start(bf16[8,256,512]{2,1,0:T(8,128)(2,1)} %copy.27) | copy-start | bytes 6291460
  154.6 1.3 copy-start.1
  218.0 4.1 copy-start.5
  268.8 1.3 copy-start.3
  333.0 4.1 copy-start.6
  383.7 1.4 copy-start.2
  423.6 33.4 %copy-start.7 = (f32[256,512]{1,0:T(8,128)S(1)}, f32[256,512]{1,0:T(8,128)}, u32[]{:S(2)}) copy-start(f32[256,512]{1,0:T(8,128)} %get-tuple-element.88) | copy-start | bytes 1572868
